TPU v7x, 512 devices: a whole 4x8x8 slice. The times are simulated.
512 devices in a mesh: freq: 16 (over z_lo, x), tm: 32 (over z_hi, y, core).
Axes of the slice: x: 4, y: 8, z: 8 (z_hi: 2, z_lo: 4; z = z_hi * 4 + z_lo), core: 2. Of those that a mesh axis runs over, the one named last changes fastest.
Arguments:
- baseband: bfloat16 [128, 4, 262144], P('freq', None, 'tm'), may hold values from -3 to 3
- chirp_phase: float32 [128, 16384], P('freq'), may hold values from -3.140625 to 3.140625
- phase_bins: int32 [262144], P('tm'), may hold values from 0 to 1023
Outputs:
- profile: float32 [128, 4, 1024], P('freq', None, 'tm')
Inputs may be any that keep to these rules, and one draw needn't show every extreme that they name: `phase_bins`: each time sample's phase bin.
All inputs are finite; a program needn't handle non-finite values.
Results may differ from a plain program's by a relative error of at most 0.0003.
Values may be sent and summed in bfloat16 or wider, within the bound.
A program may use at most 64 MiB of HBM per device.

v0:
```python
import math
import jax
import jax.numpy as jnp
from jax import lax
from jax.sharding import PartitionSpec as P

BINS = 1024


def shifted(block, axis, distance):
    devices = range(lax.axis_size(axis))
    route = [(i - distance, i) for i in devices if i - distance in devices]
    return lax.ppermute(block, axis, route)


def dft_tables(radix_size):
    indices = jnp.arange(radix_size, dtype=jnp.int32)
    product_small = indices[:, None] * indices[None, :] % radix_size
    angles = product_small.astype(jnp.float32) * (2.0 * math.pi / radix_size)
    product_large = indices[:, None] * indices[None, :] % (radix_size * radix_size)
    twists = product_large.astype(jnp.float32) * (2.0 * math.pi / (radix_size * radix_size))
    return (jnp.cos(angles), -jnp.sin(angles), jnp.cos(twists), -jnp.sin(twists))


def left_product(matrix_real, matrix_imag, vector_real, vector_imag):

    def apply(matrix, vector):
        return jnp.einsum("kn,cpsnm->cpskm", matrix, vector, precision=lax.Precision.HIGH)

    return (
        apply(matrix_real, vector_real) - apply(matrix_imag, vector_imag),
        apply(matrix_real, vector_imag) + apply(matrix_imag, vector_real),
    )


def right_product(vector_real, vector_imag, matrix_real, matrix_imag):

    def apply(vector, matrix):
        return jnp.einsum("cpskn,nm->cpskm", vector, matrix, precision=lax.Precision.HIGH)

    return (
        apply(vector_real, matrix_real) - apply(vector_imag, matrix_imag),
        apply(vector_real, matrix_imag) + apply(vector_imag, matrix_real),
    )


def filter_frames(frames, response_real, response_imag, tables):
    four_real, four_imag, twist_real, twist_imag = tables
    channels, _, frame_count, frame_len = frames.shape
    radix_size = four_real.shape[0]
    keep_count = frame_len // 2
    shaped = frames.reshape(channels, 2, 2, frame_count, radix_size, radix_size)
    input_real = shaped[:, :, 0]
    input_imag = shaped[:, :, 1]
    section_real, section_imag = left_product(four_real, four_imag, input_real, input_imag)
    turned_real = section_real * twist_real - section_imag * twist_imag
    turned_imag = section_real * twist_imag + section_imag * twist_real
    spec_real, spec_imag = right_product(turned_real, turned_imag, four_real, four_imag)
    gain_real = response_real[:, None, None]
    gain_imag = response_imag[:, None, None]
    shaped_real = spec_real * gain_real - spec_imag * gain_imag
    shaped_imag = spec_real * gain_imag + spec_imag * gain_real
    back_real, back_imag = right_product(shaped_real, shaped_imag, four_real, -four_imag)
    untwist_real = back_real * twist_real + back_imag * twist_imag
    untwist_imag = back_imag * twist_real - back_real * twist_imag
    wave_real, wave_imag = left_product(four_real, -four_imag, untwist_real, untwist_imag)
    factor = 1.0 / frame_len
    wave_real = wave_real.reshape(channels, 2, frame_count, frame_len)[..., keep_count:] * factor
    wave_imag = wave_imag.reshape(channels, 2, frame_count, frame_len)[..., keep_count:] * factor
    return (wave_real, wave_imag)


def fold_blocks(stokes, phase_bins):
    channels, _, samples = stokes.shape
    width = min(1024, samples)
    count = samples // width
    bin_ids = jnp.arange(BINS, dtype=jnp.int32)

    def add_block(index, total):
        start = index * width
        part_bins = lax.dynamic_slice_in_dim(phase_bins, start, width, 0)
        part_stokes = lax.dynamic_slice_in_dim(stokes, start, width, 2)
        onehot = (part_bins[:, None] == bin_ids[None, :]).astype(jnp.float32)
        return total + jnp.einsum("cjt,tb->cjb", part_stokes, onehot, precision=lax.Precision.HIGH)

    return lax.fori_loop(0, count, add_block, jnp.zeros((channels, 4, BINS), jnp.float32))


def shards(baseband, chirp_phase, phase_bins):
    channels, _, samples = baseband.shape
    frame_len = chirp_phase.shape[1]
    keep_count = frame_len // 2
    radix_size = math.isqrt(frame_len)
    segments = samples // keep_count
    tables = dft_tables(radix_size)
    turned = chirp_phase.reshape(channels, radix_size, radix_size).transpose(0, 2, 1)
    response_real = jnp.cos(turned)
    response_imag = jnp.sin(turned)
    rim_samples = shifted(baseband, "tm", 1)
    extended = jnp.concatenate([rim_samples, baseband], axis=2).astype(jnp.float32)
    blocks = extended.reshape(channels, 4, segments + 1, keep_count)
    frames = jnp.concatenate([blocks[:, :, :-1], blocks[:, :, 1:]], axis=3)
    wave_real, wave_imag = filter_frames(frames, response_real, response_imag, tables)
    first_real = wave_real[:, 0].reshape(channels, samples)
    first_imag = wave_imag[:, 0].reshape(channels, samples)
    second_real = wave_real[:, 1].reshape(channels, samples)
    second_imag = wave_imag[:, 1].reshape(channels, samples)
    power_first = first_real * first_real + first_imag * first_imag
    power_second = second_real * second_real + second_imag * second_imag
    stokes = jnp.stack(
        [
            power_first + power_second,
            power_first - power_second,
            2.0 * (first_real * second_real + first_imag * second_imag),
            2.0 * (first_real * second_imag - first_imag * second_real),
        ],
        axis=1,
    )
    folded = fold_blocks(stokes, phase_bins)
    factor = 1.0 / float(samples * lax.axis_size("tm") // BINS)
    summed = lax.psum(folded, "tm")
    part_width = BINS // lax.axis_size("tm")
    profile_part = lax.dynamic_slice_in_dim(
        summed, lax.axis_index("tm") * part_width, part_width, 2
    )
    return profile_part * factor


def solution(mesh):
    placed = (P("freq", None, "tm"), P("freq", None), P("tm"))
    return jax.shard_map(
        shards, mesh=mesh, in_specs=placed, out_specs=P("freq", None, "tm"), check_vma=False
    )
```

profile of v0, /device:TPU:1, one launch (start us, length us, event | category | flops | bytes accessed | tf_op | source)
XLA Modules:
  0.0 407.9 jit_solution(17535864532734620487)
XLA Ops:
  6.5 4.7 %collective-permute-start = (bf16[8,4,8192]{2,1,0:T(4,128)(2,1)}, bf16[8,4,8192]{2,1,0:T(4,128)(2,1)S(1)}, u32[]{:S(2)}, u32[]{:S(2)}) collective-permute-start(bf16[8,4,8192]{2,1,0:T(4,128)(2,1)} %param.5), channel_id=1, source_target_pairs={{0,1},{1,2},{2,3},{3,4},{4,5},{5,6},{6,7},{7,8},{8,9},{9,10},{10,1... | collective-permute-start | bytes 1572872 | tf_op jit(solution)/shard_map/ppermute | solution.py:13
  11.7 2.8 cosine_bitcast_fusion
  15.0 2.7 collective-permute-done
  18.5 1.8 pad_maximum_fusion
  20.3 2.9 reshape.302
  23.2 1.1 fusion.21
  24.3 1.1 fusion.22
  25.4 1.1 fusion.14
  26.6 1.1 fusion.13
  27.7 1.2 fusion.19
  28.9 1.2 fusion.17
  30.1 1.2 convolution_subtract_fusion.2
  31.4 1.2 convolution_add_fusion.2
  34.5 1.1 convolution_add_fusion.1
  36.6 1.2 fusion.23
  37.7 1.2 fusion.24
  38.9 2.2 fusion.12
  41.1 2.6 copy.56
  44.8 1.1 copy_multiply_fusion.1
  45.9 2.2 fusion.11
  48.1 1.6 copy.60
  50.3 16.3 %while.14 = (s32[]{:T(128)}, f32[8,4,1024]{2,0,1:T(8,128)S(1)}, f32[8,4,8192]{2,0,1:T(8,128)S(1)}, s32[8192]{0:T(1024)}, s32[]{:T(128)}, /*index=5*/s32[]{:T(128)}, s32[]{:T(128)}, s32[]{:T(128)}) while((s32[]{:T(128)}, f32[8,4,1024]{2,0,1:T(8,128)S(1)}, f32[8,4,8192]{2,0,1:T(8,128)S(1)}, s32[8192]{0:T(1024)}, s32[]{:T(128)}, ...), condition=%wide.region_1.2_spmd.clone, body=%wide.region_0.1_spmd.clone.sunk | while | flops 202440704 | bytes 405653 | solution.py:86
  51.0 1.3 fusion.147
  53.1 1.3 fusion.147
  55.1 1.3 fusion.147
  57.1 1.3 fusion.147
  59.2 1.3 fusion.147
  61.2 1.3 fusion.147
  63.2 1.3 fusion.147
  65.3 1.3 fusion.147
  67.4 332.3 %all-reduce.2.cloned.1.call-done = f32[8,4,1024]{2,1,0:T(4,128)} async-done(((f32[8,4,1024]{2,1,0:T(4,128)}), f32[8,4,1024]{2,1,0:T(4,128)}) %all-reduce.2.cloned.1.call-update) | async-done | bytes 131088 | tf_op jit(solution)/shard_map/psum | solution.py:121
  399.7 1.4 dynamic-slice_multiply_fusion
  (31 shorter events, 12.5 us)
Async XLA Ops:
  6.5 11.1 %copy-start.1 = (bf16[8,4,8192]{2,1,0:T(4,128)(2,1)S(1)}, bf16[8,4,8192]{2,1,0:T(4,128)(2,1)}, u32[]{:S(2)}) copy-start(bf16[8,4,8192]{2,1,0:T(4,128)(2,1)} %param.5) | copy-start | bytes 1572868
  6.5 393.1 %all-reduce.2.cloned.1.call-start = ((), (), s32[]{:S(2)}) async-start(), calls=%async_computation | async-start | bytes 262144 | tf_op jit(solution)/shard_map/psum | solution.py:121
  6.5 11.1 %collective-permute-start = (bf16[8,4,8192]{2,1,0:T(4,128)(2,1)}, bf16[8,4,8192]{2,1,0:T(4,128)(2,1)S(1)}, u32[]{:S(2)}, u32[]{:S(2)}) collective-permute-start(bf16[8,4,8192]{2,1,0:T(4,128)(2,1)} %param.5), channel_id=1, source_target_pairs={{0,1},{1,2},{2,3},{3,4},{4,5},{5,6},{6,7},{7,8},{8,9},{9,10},{10,1... | collective-permute-start | bytes 1572872 | tf_op jit(solution)/shard_map/ppermute | solution.py:13
  48.1 2.0 copy-start
Sparse Core Ops, SparseCore 0:
  67.5 332.1 all-reduce.1
where the time goes:
time: 408 us
  waiting for transfers between devices  335 us (82%)
  matrix products  30.5 us (7%)
  local copies, waits for them, and re-layouts  18.1 us (4%)
  between operations  13.6 us (3%)
  other arithmetic  5.86 us (1%)
  starting transfers between devices  4.7 us (1%)
    psum x1, waiting for transfers between devices, shards(): summed = lax.psum(folded, 'tm')  332 us
    dot_general x8, matrix products, apply(): jnp.einsum('kn,cpsnm->cpskm', matrix, vector, precision=lax.Precision.HIGH)  11.1 us
    dot_general x8, matrix products, add_block(): jnp.einsum('cjt,tb->cjb', part_stokes, onehot, precision=lax.Precision.HIGH)  10.5 us
    dot_general x8, matrix products, apply(): jnp.einsum('cpskn,nm->cpskm', vector, matrix, precision=lax.Precision.HIGH)  8.81 us
  transfers between devices with their start and end apart: 2, of which 2 were waited for; matrix products, arithmetic and copies ran while one was open for 1% of the time, Pallas kernels for 0%

commit v1 on v0

--- a/solution.py
+++ b/solution.py
@@ -118,7 +118,7 @@
     )
     folded = fold_blocks(stokes, phase_bins)
     factor = 1.0 / float(samples * lax.axis_size("tm") // BINS)
-    summed = lax.psum(folded, "tm")
+    summed = jnp.sum(lax.all_gather(folded, "tm"), axis=0)
     part_width = BINS // lax.axis_size("tm")
     profile_part = lax.dynamic_slice_in_dim(
         summed, lax.axis_index("tm") * part_width, part_width, 2

time: 408 us -> 197 us (0.48)
  waiting for transfers between devices: 335 us -> 122 us
    psum x1 -> x0, waiting for transfers between devices: 332 us -> none  [shards(): summed = lax.psum(folded, 'tm')]
    all_gather x0 -> x1, waiting for transfers between devices: none -> 119 us  [shards(): summed = jnp.sum(lax.all_gather(folded, 'tm'), axis=0)]
  transfers between devices with their start and end apart: 2 -> 2, of which waited for: 2 -> 2; matrix products, arithmetic and copies ran while one was open for 1% -> 2% of each run, Pallas kernels for 0% -> 0%
where the time goes in v1:
time: 197 us; the launch traced here: 196 us
  waiting for transfers between devices  122 us (62%)
  matrix products  30.4 us (15%)
  local copies, waits for them, and re-layouts  18.6 us (9%)
  between operations  13.6 us (7%)
  other arithmetic  6.99 us (4%)
  starting transfers between devices  4.7 us (2%)
    all_gather x1, waiting for transfers between devices, shards(): summed = jnp.sum(lax.all_gather(folded, 'tm'), axis=0)  119 us
    dot_general x8, matrix products, apply(): jnp.einsum('kn,cpsnm->cpskm', matrix, vector, precision=lax.Precision.HIGH)  11.1 us
    dot_general x8, matrix products, add_block(): jnp.einsum('cjt,tb->cjb', part_stokes, onehot, precision=lax.Precision.HIGH)  10.5 us
    dot_general x8, matrix products, apply(): jnp.einsum('cpskn,nm->cpskm', vector, matrix, precision=lax.Precision.HIGH)  8.81 us
    dynamic_slice x8, local copies, waits for them, and re-layouts, add_block(): part_bins = lax.dynamic_slice_in_dim(phase_bins, start, width, 0)  5.54 us
    ppermute x1, starting transfers between devices, shifted(): return lax.ppermute(block, axis, route)  4.7 us
  transfers between devices with their start and end apart: 2, of which 2 were waited for; matrix products, arithmetic and copies ran while one was open for 2% of the time, Pallas kernels for 0%

profile of v1, /device:TPU:1, one launch (start us, length us, event | category | flops | bytes accessed | tf_op | source)
XLA Modules:
  0.0 196.4 jit_solution(15029913440367421625)
XLA Ops:
  6.5 4.7 %collective-permute-start = (bf16[8,4,8192]{2,1,0:T(4,128)(2,1)}, bf16[8,4,8192]{2,1,0:T(4,128)(2,1)S(1)}, u32[]{:S(2)}, u32[]{:S(2)}) collective-permute-start(bf16[8,4,8192]{2,1,0:T(4,128)(2,1)} %param.5), channel_id=1, source_target_pairs={{0,1},{1,2},{2,3},{3,4},{4,5},{5,6},{6,7},{7,8},{8,9},{9,10},{10,1... | collective-permute-start | bytes 1572872 | tf_op jit(solution)/shard_map/ppermute | solution.py:13
  11.7 2.8 %cosine_bitcast_fusion = (f32[8,128,128]{2,0,1:T(8,128)S(1)}, f32[8,128,128]{2,0,1:T(8,128)S(1)}) fusion(f32[8,16384]{1,0:T(8,128)} %param.6), kind=kLoop, calls=%fused_computation.43 | loop fusion | bytes 1572864 | tf_op jit(solution)/shard_map/cos | solution.py:97
  15.0 2.7 %collective-permute-done = bf16[8,4,8192]{2,1,0:T(4,128)(2,1)S(1)} collective-permute-done((bf16[8,4,8192]{2,1,0:T(4,128)(2,1)}, bf16[8,4,8192]{2,1,0:T(4,128)(2,1)S(1)}, u32[]{:S(2)}, u32[]{:S(2)}) %collective-permute-start) | collective-permute-done | bytes 524320 | tf_op jit(solution)/shard_map/ppermute | solution.py:13
  18.5 1.8 pad_maximum_fusion
  20.3 2.9 %reshape.302 = f32[8,2,2,1,128,128]{5,4,3,2,1,0:T(8,128)S(1)} reshape(f32[8,4,1,16384]{3,1,0,2:T(4,128)} %pad_maximum_fusion) | data formatting | bytes 4194304 | tf_op jit(solution)/shard_map/reshape | solution.py:52
  23.2 1.1 fusion.21
  24.3 1.1 fusion.22
  25.4 1.1 fusion.14
  26.5 1.1 fusion.13
  27.7 1.2 fusion.19
  28.9 1.2 fusion.17
  30.1 1.2 convolution_subtract_fusion.2
  31.4 1.2 convolution_add_fusion.2
  34.4 1.1 convolution_add_fusion.1
  36.5 1.2 fusion.23
  37.7 1.2 fusion.24
  38.9 2.2 %fusion.12 = f32[8,2,1,128,128]{3,4,1,0,2:T(8,128)} fusion(f32[8,2,128,128]{3,2,1,0:T(8,128)S(1)} %fusion.23, f32[8,2,128,128]{3,2,1,0:T(8,128)S(1)} %convolution_subtract_fusion.1, f32[8,2,128,128]{3,2,1,0:T(8,128)S(1)} %convolution_add_fusion.1, f32[128,128]{1,0:T(8,128)S(1)} %get-tuple-element.141, f32[128,128]{1,0:T(8,128)S(1)} %get-tuple-element.142), kind=kOutput, calls=%fused_computation.13 | convolution fusion | flops 202604544 | bytes 4325376 | tf_op jit(solution)/shard_map/kn,cpsnm->cpskm/dot_general | solution.py:28
  41.1 2.6 %copy.81 = f32[8,2,1,128,128]{4,3,2,1,0:T(8,128)} copy(f32[8,2,1,128,128]{3,4,1,0,2:T(8,128)} %fusion.12) | data formatting | bytes 2097152 | tf_op jit(solution)/shard_map/sub | solution.py:31
  44.7 1.2 copy_multiply_fusion.1
  45.9 2.2 %fusion.11 = f32[8,2,1,128,128]{3,4,1,0,2:T(8,128)} fusion(f32[8,2,128,128]{3,2,1,0:T(8,128)S(1)} %fusion.24, f32[8,2,128,128]{3,2,1,0:T(8,128)S(1)} %convolution_add_fusion.1, f32[8,2,128,128]{3,2,1,0:T(8,128)S(1)} %convolution_subtract_fusion.1, f32[128,128]{1,0:T(8,128)S(1)} %get-tuple-element.141, f32[128,128]{1,0:T(8,128)S(1)} %get-tuple-element.142), kind=kOutput, calls=%fused_computation.11 | convolution fusion | flops 202604544 | bytes 4325376 | tf_op jit(solution)/shard_map/kn,cpsnm->cpskm/dot_general | solution.py:28
  48.0 1.6 copy.85
  50.3 16.3 %while.14 = (s32[]{:T(128)}, f32[8,4,1024]{2,0,1:T(8,128)S(1)}, f32[8,4,8192]{2,0,1:T(8,128)S(1)}, s32[8192]{0:T(1024)}, s32[]{:T(128)}, /*index=5*/s32[]{:T(128)}, s32[]{:T(128)}, s32[]{:T(128)}) while((s32[]{:T(128)}, f32[8,4,1024]{2,0,1:T(8,128)S(1)}, f32[8,4,8192]{2,0,1:T(8,128)S(1)}, s32[8192]{0:T(1024)}, s32[]{:T(128)}, ...), condition=%wide.region_1.2_spmd.clone, body=%wide.region_0.1_spmd.clone.sunk | while | flops 202440704 | bytes 405653 | solution.py:86
  51.0 1.3 fusion.147
  53.1 1.3 fusion.147
  55.1 1.3 fusion.147
  57.1 1.3 fusion.147
  59.2 1.3 fusion.147
  61.2 1.3 fusion.147
  63.2 1.3 fusion.147
  65.3 1.3 fusion.147
  67.3 119.2 %all-gather.3.cloned.1.call-done = f32[256,4,1024]{2,0,1:T(8,128)} async-done(((f32[8,4,1024]{2,0,1:T(8,128)}), f32[256,4,1024]{2,0,1:T(8,128)}) %all-gather.3.cloned.1.call-update) | async-done | bytes 4194320 | tf_op jit(solution)/shard_map/all_gather | solution.py:121
  186.4 2.4 %bitcast_reduce_fusion = f32[8,4,1024]{2,0,1:T(8,128)S(1)} fusion(f32[256,4,1024]{2,0,1:T(8,128)} %all-gather.3.cloned.1.call-done), kind=kLoop, calls=%fused_computation.8 | loop fusion | flops 1015808 | bytes 4325376 | tf_op jit(solution)/shard_map/reduce_sum | solution.py:121
  (34 shorter events, 13.1 us)
Async XLA Ops:
  6.5 11.1 %copy-start.1 = (bf16[8,4,8192]{2,1,0:T(4,128)(2,1)S(1)}, bf16[8,4,8192]{2,1,0:T(4,128)(2,1)}, u32[]{:S(2)}) copy-start(bf16[8,4,8192]{2,1,0:T(4,128)(2,1)} %param.5) | copy-start | bytes 1572868
  6.5 179.9 %all-gather.3.cloned.1.call-start = ((), (), s32[]{:S(2)}) async-start(), calls=%async_computation | async-start | bytes 4325376 | tf_op jit(solution)/shard_map/all_gather | solution.py:121
  6.5 11.1 %collective-permute-start = (bf16[8,4,8192]{2,1,0:T(4,128)(2,1)}, bf16[8,4,8192]{2,1,0:T(4,128)(2,1)S(1)}, u32[]{:S(2)}, u32[]{:S(2)}) collective-permute-start(bf16[8,4,8192]{2,1,0:T(4,128)(2,1)} %param.5), channel_id=1, source_target_pairs={{0,1},{1,2},{2,3},{3,4},{4,5},{5,6},{6,7},{7,8},{8,9},{9,10},{10,1... | collective-permute-start | bytes 1572872 | tf_op jit(solution)/shard_map/ppermute | solution.py:13
  48.0 2.0 %copy-start = (f32[8,2,1,8192]{3,0,2,1:T(8,128)S(1)}, f32[8,2,1,8192]{3,0,2,1:T(8,128)}, u32[]{:S(2)}) copy-start(f32[8,2,1,8192]{3,0,2,1:T(8,128)} %copy_multiply_fusion.1) | copy-start | bytes 1572868
  66.6 0.6 copy-start.2
Sparse Core Ops, SparseCore 0:
  67.4 118.9 all-gather.2
